TPU v7x, 128 devices: a whole 4x4x4 slice. The times are simulated.
128 devices in a mesh: tok: 8 (over z, core), head: 16 (over y, x).
Axes of the slice: x: 4, y: 4, z: 4, core: 2. Of those that a mesh axis runs over, the one named last changes fastest.
Arguments:
- stream: bfloat16 [2048, 7168], P('tok'), may hold values from -400 to 400
- row_tree_nodes: int32 [2048], replicated, may hold values from 0 to 2047, as said below
- input_norm_gain: bfloat16 [7168], replicated, may hold values from 0.099609375 to 1.8984375
- query_key_value_weight: bfloat16 [7168, 3, 7168], P('head', None, 'tok'), may hold values from -0.141736677 to 0.141736677
- adapter_down_weight: bfloat16 [7168, 128], replicated, may hold values from -0.0625 to 0.0625
- adapter_up_weight: bfloat16 [128, 3, 7168], P('head', None, 'tok'), may hold values from -0.23925781 to 0.23925781
- key_value_cache: bfloat16 [2, 32, 2048, 7168], P(None, 'head', None, 'tok'), may hold values from -104 to 104
- cache_length: int32 [32], P('head'), may hold values from 256 to 2048, as said below
- parents: int32 [32, 64], P('head'), may hold values from 0 to 62, as said below
- accepted: int32 [32, 8], P('head'), may hold values from 0 to 63, as said below
- output_weight: bfloat16 [7168, 3584], P('tok', 'head'), may hold values from -0.375 to 0.375
Outputs:
- attended: bfloat16 [2048, 3584], P('tok', 'head')
- accepted_kv: bfloat16 [2, 32, 8, 7168], P(None, 'head', None, 'tok')
Inputs may be any that keep to these rules, and one draw needn't show every extreme that they name: row_tree_nodes is a permutation of the 2048 node numbers; every aligned block of 128 rows holds exactly 4 nodes of every request. `cache_length`: at least one request's cache holds exactly 2048 positions. parents[r, 0] = 0 marks the root; parents[r, n] < n for n > 0. `accepted`: each row lists 8 nodes of its request's tree, each the parent of the next.
All inputs are finite; a program needn't handle non-finite values.
Results may differ from a plain program's by a relative error of at most 0.014.
Values may be sent and summed in bfloat16 or wider, within the bound.
A program may use at most 192 MiB of HBM per device.

v0:
```python
import jax
import jax.numpy as jnp
from jax import lax
from jax.sharding import PartitionSpec as P

HEAD_SIZE = 224
NODES = 64


def ancestors_of(parents):
    parent_links = jax.nn.one_hot(parents, NODES, dtype=jnp.float32)
    identity_matrix = jnp.eye(NODES, dtype=jnp.float32)
    ancestry = jnp.minimum(identity_matrix[None] + parent_links, 1.0)
    for squaring in range(NODES.bit_length()):
        ancestry = jnp.minimum(
            jnp.einsum("rnm,rmk->rnk", ancestry, ancestry, precision=lax.Precision.HIGHEST), 1.0
        )
    return ancestry


def on_device(
    stream,
    row_tree_nodes,
    input_norm_gain,
    query_key_value_weight,
    adapter_down_weight,
    adapter_up_weight,
    key_value_cache,
    cache_length,
    parents,
    accepted,
    output_weight,
):
    owner_index = lax.axis_index("head")
    feature_rows = query_key_value_weight.shape[0]
    device_width = query_key_value_weight.shape[2]
    adapter_rank_rows = adapter_up_weight.shape[0]
    local_heads = device_width // HEAD_SIZE
    request_count = key_value_cache.shape[1]
    cache_span = key_value_cache.shape[2]
    wide_rows = stream.astype(jnp.float32)
    inverse_rms = lax.rsqrt(jnp.mean(wide_rows * wide_rows, axis=1, keepdims=True) + 1e-05)
    normalized_input = (wide_rows * inverse_rms * input_norm_gain.astype(jnp.float32)).astype(
        jnp.bfloat16
    )
    reduced_rank_rows = jnp.dot(
        normalized_input, adapter_down_weight, preferred_element_type=jnp.float32
    ).astype(jnp.bfloat16)
    feature_block = lax.dynamic_slice_in_dim(
        normalized_input, owner_index * feature_rows, feature_rows, 1
    )
    rank_block = lax.dynamic_slice_in_dim(
        reduced_rank_rows, owner_index * adapter_rank_rows, adapter_rank_rows, 1
    )
    gathered_features, gathered_ranks = (
        lax.all_gather(feature_block, "tok", axis=0, tiled=True),
        lax.all_gather(rank_block, "tok", axis=0, tiled=True),
    )
    projection = query_key_value_weight.reshape(feature_rows, 3 * device_width)
    lifting_matrix = adapter_up_weight.reshape(adapter_rank_rows, 3 * device_width)
    node_to_row = jnp.argsort(row_tree_nodes)
    part_sum = jnp.dot(
        gathered_features[node_to_row], projection, preferred_element_type=jnp.float32
    )
    node_rows = lax.psum_scatter(
        part_sum
        + jnp.dot(gathered_ranks[node_to_row], lifting_matrix, preferred_element_type=jnp.float32),
        "head",
        scatter_dimension=0,
        tiled=True,
    ).astype(jnp.bfloat16)
    triple = node_rows.reshape(request_count, NODES, 3, local_heads, HEAD_SIZE)
    queries = triple[:, :, 0]
    tree_key_rows = triple[:, :, 1]
    tree_value_rows = triple[:, :, 2]
    ancestry = ancestors_of(parents)
    attention_score_scale = HEAD_SIZE ** (-0.5)
    tree_score_matrix = (
        jnp.einsum("rnhd,rmhd->rhnm", queries, tree_key_rows, preferred_element_type=jnp.float32)
        * attention_score_scale
    )
    tree_score_matrix = jnp.where(ancestry[:, None] > 0.5, tree_score_matrix, -jnp.inf)
    keys_cache = key_value_cache[0].reshape(request_count, cache_span, local_heads, HEAD_SIZE)
    values_cache = key_value_cache[1].reshape(request_count, cache_span, local_heads, HEAD_SIZE)
    scores = (
        jnp.einsum("rnhd,rchd->rhnc", queries, keys_cache, preferred_element_type=jnp.float32)
        * attention_score_scale
    )
    positions = lax.broadcasted_iota(jnp.int32, (1, 1, 1, cache_span), 3)
    scores = jnp.where(positions < cache_length[:, None, None, None], scores, -jnp.inf)
    tree_top = jnp.max(tree_score_matrix, axis=-1, keepdims=True)
    largest = jnp.maximum(tree_top, jnp.max(scores, axis=-1, keepdims=True))
    cache_exp = jnp.exp(scores - largest)
    tree_exp = jnp.exp(tree_score_matrix - largest)
    totals = jnp.sum(cache_exp, axis=-1, keepdims=True) + jnp.sum(tree_exp, axis=-1, keepdims=True)
    cache_weights = (cache_exp / totals).astype(jnp.bfloat16)
    tree_weight_matrix = (tree_exp / totals).astype(jnp.bfloat16)
    attention = jnp.einsum(
        "rhnc,rchd->rnhd", cache_weights, values_cache, preferred_element_type=jnp.float32
    )
    attention = attention + jnp.einsum(
        "rhnm,rmhd->rnhd", tree_weight_matrix, tree_value_rows, preferred_element_type=jnp.float32
    )
    head_rows = attention.astype(jnp.bfloat16).reshape(request_count * NODES, device_width)
    node_table = node_rows.reshape(request_count, NODES, 3, device_width)
    chosen = jnp.take_along_axis(node_table, accepted[:, :, None, None], axis=1)
    accepted_kv = jnp.stack([chosen[:, :, 1], chosen[:, :, 2]])
    everything = lax.all_gather(head_rows, "head", axis=0, tiled=True)
    attended = lax.psum_scatter(
        jnp.dot(
            everything[row_tree_nodes], output_weight, preferred_element_type=jnp.float32
        ).astype(jnp.bfloat16),
        "tok",
        scatter_dimension=0,
        tiled=True,
    )
    return (attended, accepted_kv)


def solution(mesh):
    placed = (
        P("tok", None),
        P(),
        P(),
        P("head", None, "tok"),
        P(),
        P("head", None, "tok"),
        P(None, "head", None, "tok"),
        P("head"),
        P("head", None),
        P("head", None),
        P("tok", "head"),
    )
    return jax.shard_map(
        on_device,
        mesh=mesh,
        in_specs=placed,
        out_specs=(P("tok", "head"), P(None, "head", None, "tok")),
        check_vma=False,
    )
```

profile of v0, /device:TPU:0, one launch (start us, length us, event | category | flops | bytes accessed | tf_op | source)
XLA Modules:
  0.0 344.5 jit_solution(10668677327071454545)
XLA Ops:
  7.2 0.8 convert_element_type.39
  8.1 2.8 fusion
  10.9 3.1 fusion.2
  14.0 1.8 copy-done.2
  15.8 0.9 constant_dynamic-slice_fusion
  16.7 4.5 %copy.21 = bf16[448,3,896]{0,2,1:T(8,128)(2,1)} copy(bf16[448,3,896]{2,0,1:T(8,128)(2,1)} %param.14) | data formatting | bytes 4816896 | tf_op args[3]
  21.2 5.0 %sort.17 = (s32[2048]{0:T(1024)}, s32[2048]{0:T(1024)S(1)}) sort(s32[2048]{0:T(1024)S(1)} %copy-done.4, s32[2048]{0:T(1024)S(1)} %iota.34), dimensions={0}, to_apply=%region_1.0 | sort | flops 22528 | bytes 32768 | tf_op jit(solution)/shard_map/jit(argsort)/sort | solution.py:61
  26.3 3.2 fusion.32
  29.6 15.4 %all_gather.10 = bf16[2048,8]{1,0:T(8,128)(2,1)S(1)} all-gather(bf16[256,8]{1,0:T(8,128)(2,1)S(1)} %dynamic-slice_convert_fusion), channel_id=1, replica_groups=mesh['tok'=8,'head'=16] {'tok'}, dimensions={0}, use_global_device_ids=true | all-gather | bytes 36864 | tf_op jit(solution)/shard_map/all_gather | solution.py:57
  45.0 6.2 %gather_fusion.1 = bf16[2048,8]{1,0:T(8,128)(2,1)S(1)} fusion(bf16[2048,8]{1,0:T(8,128)(2,1)S(1)} %all_gather.10, s32[2048]{0:T(1024)S(1)} %fusion.23), kind=kCustom, calls=%fused_computation.1 | custom fusion | bytes 73728 | tf_op jit(solution)/shard_map/gather | solution.py:67
  51.2 11.1 %gather_fusion = bf16[2048,448]{1,0:T(8,128)(2,1)} fusion(bf16[2048,448]{1,0:T(8,128)(2,1)} %all-gather.3.cloned.1.call-done, s32[2048]{0:T(1024)S(1)} %fusion.23), kind=kCustom, calls=%fused_computation | custom fusion | bytes 3678208 | tf_op jit(solution)/shard_map/gather | solution.py:63
  62.3 12.6 %fusion.31 = f32[2048,2688]{1,0:T(8,128)} fusion(bf16[2048,448]{1,0:T(8,128)(2,1)} %gather_fusion, bf16[448,2688]{0,1:T(8,128)(2,1)} %bitcast.63), kind=kOutput, calls=%fused_computation.71 | convolution fusion | flops 4932501504 | bytes 26263552 | tf_op jit(solution)/shard_map/dot_general | solution.py:62
  74.9 14.2 %convolution_add_fusion = f32[2048,2688]{1,0:T(8,128)} fusion(f32[2048,2688]{1,0:T(8,128)} %fusion.31, bf16[2048,8]{1,0:T(8,128)(2,1)S(1)} %gather_fusion.1, bf16[8,2688]{1,0:T(8,128)(2,1)S(1)} %bitcast.65), kind=kOutput, calls=%fused_computation.4 | convolution fusion | flops 93585408 | bytes 44115968 | tf_op jit(solution)/shard_map/dot_general | solution.py:67
  89.4 0.4 copy-done.5
  89.8 0.3 convolution_minimum_fusion.6
  91.4 10.6 %fusion.28 = (bf16[1,2,2048,896]{3,2,1,0:T(8,128)(2,1)}, bf16[1,2,2048,896]{3,2,1,0:T(8,128)(2,1)}) fusion(bf16[2,2,2048,896]{3,2,1,0:T(8,128)(2,1)} %param.17), kind=kLoop, calls=%fused_computation.68 | loop fusion | bytes 29360128 | tf_op jit(solution)/shard_map/slice | solution.py:83
  102.0 11.3 %copy.23 = bf16[1,2,2048,896]{2,3,1,0:T(8,128)(2,1)} copy(bf16[1,2,2048,896]{3,2,1,0:T(8,128)(2,1)} %get-tuple-element.4) | data formatting | bytes 14680064 | tf_op jit(solution)/shard_map/slice | solution.py:83
  113.3 11.6 %copy.26 = bf16[1,2,2048,896]{2,3,1,0:T(8,128)(2,1)} copy(bf16[1,2,2048,896]{3,2,1,0:T(8,128)(2,1)} %get-tuple-element.5) | data formatting | bytes 14680064 | tf_op jit(solution)/shard_map/slice | solution.py:84
  124.9 102.2 %reduce-scatter.3.cloned.1.call-done = f32[128,2688]{1,0:T(8,128)} async-done(((f32[2048,2688]{1,0:T(8,128)}), f32[128,2688]{1,0:T(8,128)}) %reduce-scatter.3.cloned.1.call-update) | async-done | bytes 1376272 | tf_op jit(solution)/shard_map/reduce_scatter | solution.py:65
  227.2 1.4 convert_element_type.42
  228.6 0.9 reshape.94
  230.0 4.8 %fusion.3 = (f32[2,4,64]{2,1,0:T(4,128)S(1)}, f32[2,4,64,2048]{3,2,1,0:T(8,128)S(1)}) fusion(pred[2,2048]{1,0:T(4,128)(4,1)S(1)} %iota_compare_fusion.3, bf16[2,2048,4,224]{1,3,2,0:T(8,128)(2,1)} %bitcast.59, bf16[2,64,1,4,224]{4,3,2,1,0:T(4,128)(2,1)S(1)} %get-tuple-element.8), kind=kOutput, calls=%fused_computation.13 | convolution fusion | flops 472907264 | bytes 11769856 | tf_op jit(solution)/shard_map/rnhd,rchd->rhnc/dot_general | solution.py:86
  234.9 1.0 fusion.4
  236.0 2.5 fusion.8
  238.4 0.3 fusion.9
  238.9 0.9 reshape.95
  239.9 49.4 %all-gather.5.cloned.1.call-done = bf16[2048,896]{1,0:T(8,128)(2,1)} async-done(((bf16[128,896]{1,0:T(8,128)(2,1)}), bf16[2048,896]{1,0:T(8,128)(2,1)}) %all-gather.5.cloned.1.call-update) | async-done | bytes 3670032 | tf_op jit(solution)/shard_map/all_gather | solution.py:108
  289.3 13.1 %gather_fusion.2 = bf16[2048,896]{1,0:T(8,128)(2,1)} fusion(bf16[2048,896]{1,0:T(8,128)(2,1)} %all-gather.5.cloned.1.call-done, s32[2048]{0:T(1024)S(1)} %fusion.24), kind=kCustom, calls=%fused_computation.2 | custom fusion | bytes 7348224 | tf_op jit(solution)/shard_map/gather | solution.py:111
  302.4 4.3 %convolution_convert_fusion = bf16[2048,224]{0,1:T(8,128)(2,1)} fusion(bf16[2048,896]{1,0:T(8,128)(2,1)} %gather_fusion.2, bf16[896,224]{0,1:T(8,128)(2,1)S(1)} %copy-done.8), kind=kOutput, calls=%fused_computation.15 | convolution fusion | flops 822542336 | bytes 4988928 | tf_op jit(solution)/shard_map/dot_general | solution.py:110
  307.1 0.7 gather_fusion.3
  307.9 0.6 pad_maximum_fusion
  308.5 29.4 %reduce-scatter.5.cloned.1.call-done = bf16[256,224]{0,1:T(8,128)(2,1)} async-done(((bf16[2048,224]{0,1:T(8,128)(2,1)}), bf16[256,224]{0,1:T(8,128)(2,1)}) %reduce-scatter.5.cloned.1.call-update) | async-done | bytes 114704 | tf_op jit(solution)/shard_map/reduce_scatter | solution.py:109
  (56 shorter events, 3.1 us)
Async XLA Ops:
  7.2 19.1 %copy-start = (bf16[7168,128]{1,0:T(8,128)(2,1)S(1)}, bf16[7168,128]{1,0:T(8,128)(2,1)}, u32[]{:S(2)}) copy-start(bf16[7168,128]{1,0:T(8,128)(2,1)} %param.15) | copy-start | bytes 5505028
  7.2 44.0 %all-gather.3.cloned.1.call-start = ((), (), s32[]{:S(2)}) async-start(), calls=%async_computation.2 | async-start | bytes 2359296 | tf_op jit(solution)/shard_map/all_gather | solution.py:56
  14.0 1.8 copy-start.2
  15.8 5.4 %copy-start.4 = (s32[2048]{0:T(1024)S(1)}, s32[2048]{0:T(1024)}, u32[]{:S(2)}) copy-start(s32[2048]{0:T(1024)} %param.12) | copy-start | bytes 24580
  16.7 210.5 %reduce-scatter.3.cloned.1.call-start = ((), (), s32[]{:S(2)}) async-start(), calls=%async_computation.3 | async-start | bytes 23396352 | tf_op jit(solution)/shard_map/reduce_scatter | solution.py:65
  62.3 12.6 %copy-start.3 = (bf16[8,3,896]{2,0,1:T(8,128)(2,1)S(1)}, bf16[8,3,896]{2,0,1:T(8,128)(2,1)}, u32[]{:S(2)}) copy-start(bf16[8,3,896]{2,0,1:T(8,128)(2,1)} %param.16) | copy-start | bytes 129028
  89.1 0.7 copy-start.5
  89.1 200.2 %all-gather.5.cloned.1.call-start = ((), (), s32[]{:S(2)}) async-start(), calls=%async_computation.4 | async-start | bytes 3899392 | tf_op jit(solution)/shard_map/all_gather | solution.py:108
  113.3 11.6 %copy-start.7 = (s32[2]{0:T(128)S(1)}, s32[2]{0:T(128)}, u32[]{:S(2)}) copy-start(s32[2]{0:T(128)} %param.18) | copy-start | bytes 28
  230.0 6.0 %slice-start = ((s8[7340032]{0:T(1024)(128)(4,1)}), s8[4194304]{0:T(1024)(128)(4,1)S(1)}, s32[]{:S(2)}) async-start(s8[7340032]{0:T(1024)(128)(4,1)} %bitcast.60), calls=%async_computation.6 | async-start | bytes 8388608
  230.0 5.9 %slice-start.1 = ((s8[7340032]{0:T(1024)(128)(4,1)}), s8[3145728]{0:T(1024)(128)(4,1)S(1)}, s32[]{:S(2)}) async-start(s8[7340032]{0:T(1024)(128)(4,1)} %bitcast.60), calls=%async_computation.7 | async-start | bytes 6291456
  239.8 98.1 %reduce-scatter.5.cloned.1.call-start = ((), (), s32[]{:S(2)}) async-start(), calls=%async_computation.5 | async-start | bytes 1032192 | tf_op jit(solution)/shard_map/reduce_scatter | solution.py:109
  239.9 62.5 %copy-start.8 = (bf16[896,224]{0,1:T(8,128)(2,1)S(1)}, bf16[896,224]{0,1:T(8,128)(2,1)}, u32[]{:S(2)}) copy-start(bf16[896,224]{0,1:T(8,128)(2,1)} %param.21) | copy-start | bytes 1204228
  289.3 48.7 %copy-start.1 = (bf16[7168,128]{1,0:T(8,128)(2,1)S(1)}, bf16[7168,128]{1,0:T(8,128)(2,1)}, u32[]{:S(2)}) copy-start(bf16[7168,128]{1,0:T(8,128)(2,1)} %param.15) | copy-start | bytes 5505028
  302.4 4.4 %copy-start.6 = (s32[2,8]{1,0:T(2,128)S(1)}, s32[2,8]{1,0:T(2,128)}, u32[]{:S(2)}) copy-start(s32[2,8]{1,0:T(2,128)} %param.20) | copy-start | bytes 196
Sparse Core Ops, SparseCore 0:
  16.8 28.7 all-gather.2
  89.3 137.8 reduce-scatter.2
  240.0 49.2 all-gather.4
  306.9 31.0 reduce-scatter.4
where the time goes:
time: 345 us; the launch traced here: 344 us
  waiting for transfers between devices  181 us (52%)
  local copies, waits for them, and re-layouts  74.8 us (22%)
  matrix products  43.6 us (13%)
  blocking collectives  15.4 us (4%)
  other arithmetic  15.2 us (4%)
  between operations  14 us (4%)
    reduce_scatter x1, waiting for transfers between devices, on_device(): lax.psum_scatter(part_sum + jnp.dot(gathered_ranks[node_to_row], lifting_...  102 us
    all_gather x1, waiting for transfers between devices, on_device(): everything = lax.all_gather(head_rows, 'head', axis=0, tiled=True)  49.4 us
    reduce_scatter x1, waiting for transfers between devices, on_device(): lax.psum_scatter(jnp.dot(everything[row_tree_nodes], output_weight, prefe...  29.4 us
    slice x2, local copies, waits for them, and re-layouts, on_device(): key_value_cache[0]  21.9 us
    all_gather x1, blocking collectives, on_device(): lax.all_gather(rank_block, 'tok', axis=0, tiled=True)  15.4 us
    dot_general x1, matrix products, on_device(): jnp.dot(gathered_ranks[node_to_row], lifting_matrix, preferred_element_ty...  14.2 us
    gather x1, local copies, waits for them, and re-layouts, on_device(): everything[row_tree_nodes]  13.1 us
    dot_general x1, matrix products, on_device(): jnp.dot(gathered_features[node_to_row], projection, preferred_element_typ...  12.6 us
  transfers between devices with their start and end apart: 4, of which 3 were waited for; matrix products, arithmetic and copies ran while one was open for 16% of the time, Pallas kernels for 0%

commit v1 on v0

--- a/solution.py
+++ b/solution.py
@@ -5,6 +5,19 @@
 
 HEAD_SIZE = 224
 NODES = 64
+
+
+def ring_gather(x, axis, dim):
+    ways = lax.axis_size(axis)
+    up = [(d, (d + 1) % ways) for d in range(ways)]
+    down = [(d, (d - 1) % ways) for d in range(ways)]
+    earlier, later = ([x], [x])
+    for _ in range(ways // 2):
+        earlier.append(lax.ppermute(earlier[-1], axis, up))
+    for _ in range((ways - 1) // 2):
+        later.append(lax.ppermute(later[-1], axis, down))
+    line = jnp.concatenate([*earlier[::-1], *later[1:]], axis=dim)
+    return jnp.roll(line, (lax.axis_index(axis) - ways // 2) * x.shape[dim], axis=dim)
 
 
 def ancestors_of(parents):
@@ -54,7 +67,7 @@
     )
     gathered_features, gathered_ranks = (
         lax.all_gather(feature_block, "tok", axis=0, tiled=True),
-        lax.all_gather(rank_block, "tok", axis=0, tiled=True),
+        ring_gather(rank_block, "tok", 0),
     )
     projection = query_key_value_weight.reshape(feature_rows, 3 * device_width)
     lifting_matrix = adapter_up_weight.reshape(adapter_rank_rows, 3 * device_width)

time: 345 us -> 348 us (level)
  blocking collectives: 15.4 us -> 0 us
  starting transfers between devices: 0.34 us -> 9.17 us
  waiting for transfers between devices: 181 us -> 189 us
    all_gather x1 -> x0, blocking collectives: 15.4 us -> none  [on_device(): lax.all_gather(rank_block, 'tok', axis=0, tiled=True)]
    ppermute x0 -> x7, starting transfers between devices: none -> 8.83 us  [the longest x3 8.8 us: ring_gather(): later.append(lax.ppermute(later[-1], axis, down))]
    ppermute x0 -> x7, waiting for transfers between devices: none -> 7.4 us  [the longest x4 6.13 us: ring_gather(): earlier.append(lax.ppermute(earlier[-1], axis, up))]
  transfers between devices with their start and end apart: 4 -> 11, of which waited for: 3 -> 6; matrix products, arithmetic and copies ran while one was open for 16% -> 16% of each run, Pallas kernels for 0% -> 0%
where the time goes in v1:
time: 348 us; the launch traced here: 347 us
  waiting for transfers between devices  189 us (54%)
  local copies, waits for them, and re-layouts  74.5 us (21%)
  matrix products  43.8 us (13%)
  other arithmetic  16.9 us (5%)
  between operations  14.1 us (4%)
  starting transfers between devices  9.17 us (3%)
    reduce_scatter x1, waiting for transfers between devices, on_device(): lax.psum_scatter(part_sum + jnp.dot(gathered_ranks[node_to_row], lifting_...  103 us
    all_gather x1, waiting for transfers between devices, on_device(): everything = lax.all_gather(head_rows, 'head', axis=0, tiled=True)  49.4 us
    reduce_scatter x1, waiting for transfers between devices, on_device(): lax.psum_scatter(jnp.dot(everything[row_tree_nodes], output_weight, prefe...  29.4 us
    slice x2, local copies, waits for them, and re-layouts, on_device(): key_value_cache[0]  22.1 us
    dot_general x1, matrix products, on_device(): jnp.dot(gathered_ranks[node_to_row], lifting_matrix, preferred_element_ty...  14.3 us
    gather x1, local copies, waits for them, and re-layouts, on_device(): everything[row_tree_nodes]  13.1 us
    dot_general x1, matrix products, on_device(): jnp.dot(gathered_features[node_to_row], projection, preferred_element_typ...  12.6 us
    slice x1, local copies, waits for them, and re-layouts, on_device(): key_value_cache[1]  11.6 us
  transfers between devices with their start and end apart: 11, of which 6 were waited for; matrix products, arithmetic and copies ran while one was open for 16% of the time, Pallas kernels for 0%

profile of v1, /device:TPU:0, one launch (start us, length us, event | category | flops | bytes accessed | tf_op | source)
XLA Modules:
  0.0 347.4 jit_solution(270313036380042734)
XLA Ops:
  7.2 0.8 convert_element_type.39
  8.1 2.8 fusion
  10.9 4.9 %fusion.2 = bf16[256,7168]{1,0:T(8,128)(2,1)} fusion(bf16[256,7168]{1,0:T(8,128)(2,1)} %param.11, f32[7168]{0:T(1024)S(1)} %convert_element_type.39, f32[256]{0:T(256)S(1)} %add_rsqrt_fusion), kind=kLoop, calls=%fused_computation.9 | loop fusion | flops 7340032 | bytes 7369728 | tf_op jit(solution)/shard_map/convert_element_type | solution.py:56
  15.8 1.8 constant_dynamic-slice_fusion.1
  17.7 3.4 fusion.32
  21.1 4.8 %collective-permute-done = bf16[256,8]{0,1:T(8,128)(2,1)S(1)} collective-permute-done((bf16[256,8]{0,1:T(8,128)(2,1)S(1)}, bf16[256,8]{0,1:T(8,128)(2,1)S(1)}, u32[]{:S(2)}, u32[]{:S(2)}) %collective-permute-start) | collective-permute-done | bytes 4128 | tf_op jit(solution)/shard_map/ppermute | solution.py:16
  26.0 3.0 collective-permute-start.4
  28.9 1.3 collective-permute-done.1
  30.2 5.0 %sort.17 = (s32[2048]{0:T(1024)}, s32[2048]{0:T(1024)S(1)}) sort(s32[2048]{0:T(1024)S(1)} %copy-done.3, s32[2048]{0:T(1024)S(1)} %iota.34), dimensions={0}, to_apply=%region_1.2 | sort | flops 22528 | bytes 32768 | tf_op jit(solution)/shard_map/jit(argsort)/sort | solution.py:74
  35.3 3.0 collective-permute-start.5
  38.3 4.5 %copy.22 = bf16[448,3,896]{0,2,1:T(8,128)(2,1)} copy(bf16[448,3,896]{2,0,1:T(8,128)(2,1)} %param.14) | data formatting | bytes 4816896 | tf_op args[3]
  42.8 2.9 collective-permute-start.6
  45.7 1.3 collective-permute-done.6
  47.4 6.2 %gather_fusion.1 = bf16[2048,8]{1,0:T(8,128)(2,1)S(1)} fusion(bf16[2048,8]{1,0:T(8,128)(2,1)S(1)} %copy.23, s32[2048]{0:T(1024)S(1)} %fusion.23), kind=kCustom, calls=%fused_computation.1 | custom fusion | bytes 73728 | tf_op jit(solution)/shard_map/gather | solution.py:80
  53.6 11.1 %gather_fusion = bf16[2048,448]{1,0:T(8,128)(2,1)} fusion(bf16[2048,448]{1,0:T(8,128)(2,1)} %all-gather.3.cloned.1.call-done, s32[2048]{0:T(1024)S(1)} %fusion.23), kind=kCustom, calls=%fused_computation | custom fusion | bytes 3678208 | tf_op jit(solution)/shard_map/gather | solution.py:76
  64.7 12.6 %fusion.31 = f32[2048,2688]{1,0:T(8,128)} fusion(bf16[2048,448]{1,0:T(8,128)(2,1)} %gather_fusion, bf16[448,2688]{0,1:T(8,128)(2,1)} %bitcast.63), kind=kOutput, calls=%fused_computation.88 | convolution fusion | flops 4932501504 | bytes 26263552 | tf_op jit(solution)/shard_map/dot_general | solution.py:75
  77.3 14.3 %convolution_add_fusion = f32[2048,2688]{1,0:T(8,128)} fusion(f32[2048,2688]{1,0:T(8,128)} %fusion.31, bf16[2048,8]{1,0:T(8,128)(2,1)S(1)} %gather_fusion.1, bf16[8,2688]{1,0:T(8,128)(2,1)S(1)} %bitcast.65), kind=kOutput, calls=%fused_computation.4 | convolution fusion | flops 93585408 | bytes 44115968 | tf_op jit(solution)/shard_map/dot_general | solution.py:80
  93.8 10.9 %fusion.28 = (bf16[1,2,2048,896]{3,2,1,0:T(8,128)(2,1)}, bf16[1,2,2048,896]{3,2,1,0:T(8,128)(2,1)}) fusion(bf16[2,2,2048,896]{3,2,1,0:T(8,128)(2,1)} %param.17), kind=kLoop, calls=%fused_computation.85 | loop fusion | bytes 29360128 | tf_op jit(solution)/shard_map/slice | solution.py:96
  104.7 11.3 %copy.25 = bf16[1,2,2048,896]{2,3,1,0:T(8,128)(2,1)} copy(bf16[1,2,2048,896]{3,2,1,0:T(8,128)(2,1)} %get-tuple-element.4) | data formatting | bytes 14680064 | tf_op jit(solution)/shard_map/slice | solution.py:96
  116.0 11.6 %copy.28 = bf16[1,2,2048,896]{2,3,1,0:T(8,128)(2,1)} copy(bf16[1,2,2048,896]{3,2,1,0:T(8,128)(2,1)} %get-tuple-element.5) | data formatting | bytes 14680064 | tf_op jit(solution)/shard_map/slice | solution.py:97
  127.6 102.5 %reduce-scatter.3.cloned.1.call-done = f32[128,2688]{1,0:T(8,128)} async-done(((f32[2048,2688]{1,0:T(8,128)}), f32[128,2688]{1,0:T(8,128)}) %reduce-scatter.3.cloned.1.call-update) | async-done | bytes 1376272 | tf_op jit(solution)/shard_map/reduce_scatter | solution.py:78
  230.1 1.4 convert_element_type.42
  231.6 0.9 reshape.94
  233.0 4.8 %fusion.3 = (f32[2,4,64]{2,1,0:T(4,128)S(1)}, f32[2,4,64,2048]{3,2,1,0:T(8,128)S(1)}) fusion(pred[2,2048]{1,0:T(4,128)(4,1)S(1)} %iota_compare_fusion.3, bf16[2,2048,4,224]{1,3,2,0:T(8,128)(2,1)} %bitcast.59, bf16[2,64,1,4,224]{4,3,2,1,0:T(4,128)(2,1)S(1)} %get-tuple-element.8), kind=kOutput, calls=%fused_computation.13 | convolution fusion | flops 472907264 | bytes 11769856 | tf_op jit(solution)/shard_map/rnhd,rchd->rhnc/dot_general | solution.py:99
  237.9 1.0 fusion.4
  238.9 2.5 fusion.8
  241.9 0.9 reshape.95
  242.9 49.4 %all-gather.5.cloned.1.call-done = bf16[2048,896]{1,0:T(8,128)(2,1)} async-done(((bf16[128,896]{1,0:T(8,128)(2,1)}), bf16[2048,896]{1,0:T(8,128)(2,1)}) %all-gather.5.cloned.1.call-update) | async-done | bytes 3670032 | tf_op jit(solution)/shard_map/all_gather | solution.py:121
  292.2 13.1 %gather_fusion.2 = bf16[2048,896]{1,0:T(8,128)(2,1)} fusion(bf16[2048,896]{1,0:T(8,128)(2,1)} %all-gather.5.cloned.1.call-done, s32[2048]{0:T(1024)S(1)} %fusion.24), kind=kCustom, calls=%fused_computation.2 | custom fusion | bytes 7348224 | tf_op jit(solution)/shard_map/gather | solution.py:124
  305.3 4.3 %convolution_convert_fusion = bf16[2048,224]{0,1:T(8,128)(2,1)} fusion(bf16[2048,896]{1,0:T(8,128)(2,1)} %gather_fusion.2, bf16[896,224]{0,1:T(8,128)(2,1)S(1)} %copy-done.7), kind=kOutput, calls=%fused_computation.15 | convolution fusion | flops 822542336 | bytes 4988928 | tf_op jit(solution)/shard_map/dot_general | solution.py:123
  310.0 0.7 gather_fusion.3
  311.4 29.4 %reduce-scatter.5.cloned.1.call-done = bf16[256,224]{0,1:T(8,128)(2,1)} async-done(((bf16[2048,224]{0,1:T(8,128)(2,1)}), bf16[256,224]{0,1:T(8,128)(2,1)}) %reduce-scatter.5.cloned.1.call-update) | async-done | bytes 114704 | tf_op jit(solution)/shard_map/reduce_scatter | solution.py:122
  (85 shorter events, 5.0 us)
Async XLA Ops:
  7.2 10.5 %copy-start = (bf16[7168,128]{1,0:T(8,128)(2,1)S(1)}, bf16[7168,128]{1,0:T(8,128)(2,1)}, u32[]{:S(2)}) copy-start(bf16[7168,128]{1,0:T(8,128)(2,1)} %param.15) | copy-start | bytes 5505028
  7.2 46.4 %all-gather.3.cloned.1.call-start = ((), (), s32[]{:S(2)}) async-start(), calls=%async_computation.2 | async-start | bytes 2359296 | tf_op jit(solution)/shard_map/all_gather | solution.py:69
  15.8 14.4 %copy-start.3 = (s32[2048]{0:T(1024)S(1)}, s32[2048]{0:T(1024)}, u32[]{:S(2)}) copy-start(s32[2048]{0:T(1024)} %param.12) | copy-start | bytes 24580
  17.6 212.5 %reduce-scatter.3.cloned.1.call-start = ((), (), s32[]{:S(2)}) async-start(), calls=%async_computation.3 | async-start | bytes 23396352 | tf_op jit(solution)/shard_map/reduce_scatter | solution.py:78
  21.1 4.9 %collective-permute-start = (bf16[256,8]{0,1:T(8,128)(2,1)S(1)}, bf16[256,8]{0,1:T(8,128)(2,1)S(1)}, u32[]{:S(2)}, u32[]{:S(2)}) collective-permute-start(bf16[256,8]{0,1:T(8,128)(2,1)S(1)} %dynamic-slice_convert_fusion), channel_id=1, source_target_pairs={{0,16},{16,32},{32,48},{48,64},{64,80},{80,96},{96,112},{112,0},{1... | collective-permute-start | bytes 12296 | tf_op jit(solution)/shard_map/ppermute | solution.py:16
  26.0 4.2 %collective-permute-start.1 = (bf16[256,8]{0,1:T(8,128)(2,1)S(1)}, bf16[256,8]{0,1:T(8,128)(2,1)S(1)}, u32[]{:S(2)}, u32[]{:S(2)}) collective-permute-start(bf16[256,8]{0,1:T(8,128)(2,1)S(1)} %collective-permute-done), channel_id=1, source_target_pairs={{0,16},{16,32},{32,48},{48,64},{64,80},{80,96},{96,112},{112,0},{1... | collective-permute-start | bytes 12296 | tf_op jit(solution)/shard_map/ppermute | solution.py:16
  26.0 9.3 %collective-permute-start.4 = (bf16[256,8]{0,1:T(8,128)(2,1)S(1)}, bf16[256,8]{0,1:T(8,128)(2,1)S(1)}, u32[]{:S(2)}, u32[]{:S(2)}) collective-permute-start(bf16[256,8]{0,1:T(8,128)(2,1)S(1)} %dynamic-slice_convert_fusion), channel_id=1, source_target_pairs={{0,112},{16,0},{32,16},{48,32},{64,48},{80,64},{96,80},{112,96},{1... | collective-permute-start | bytes 12296 | tf_op jit(solution)/shard_map/ppermute | solution.py:18
  30.2 8.0 %collective-permute-start.2 = (bf16[256,8]{0,1:T(8,128)(2,1)S(1)}, bf16[256,8]{0,1:T(8,128)(2,1)S(1)}, u32[]{:S(2)}, u32[]{:S(2)}) collective-permute-start(bf16[256,8]{0,1:T(8,128)(2,1)S(1)} %collective-permute-done.1), channel_id=1, source_target_pairs={{0,16},{16,32},{32,48},{48,64},{64,80},{80,96},{96,112},{112,0},{1... | collective-permute-start | bytes 12296 | tf_op jit(solution)/shard_map/ppermute | solution.py:16
  35.3 7.5 %collective-permute-start.5 = (bf16[256,8]{0,1:T(8,128)(2,1)S(1)}, bf16[256,8]{0,1:T(8,128)(2,1)S(1)}, u32[]{:S(2)}, u32[]{:S(2)}) collective-permute-start(bf16[256,8]{0,1:T(8,128)(2,1)S(1)} %collective-permute-done.4), channel_id=1, source_target_pairs={{0,112},{16,0},{32,16},{48,32},{64,48},{80,64},{96,80},{112,96},{1... | collective-permute-start | bytes 12296 | tf_op jit(solution)/shard_map/ppermute | solution.py:18
  38.2 7.5 %collective-permute-start.3 = (bf16[256,8]{0,1:T(8,128)(2,1)S(1)}, bf16[256,8]{0,1:T(8,128)(2,1)S(1)}, u32[]{:S(2)}, u32[]{:S(2)}) collective-permute-start(bf16[256,8]{0,1:T(8,128)(2,1)S(1)} %collective-permute-done.2), channel_id=1, source_target_pairs={{0,16},{16,32},{32,48},{48,64},{64,80},{80,96},{96,112},{112,0},{1... | collective-permute-start | bytes 12296 | tf_op jit(solution)/shard_map/ppermute | solution.py:16
  42.8 4.2 %collective-permute-start.6 = (bf16[256,8]{0,1:T(8,128)(2,1)S(1)}, bf16[256,8]{0,1:T(8,128)(2,1)S(1)}, u32[]{:S(2)}, u32[]{:S(2)}) collective-permute-start(bf16[256,8]{0,1:T(8,128)(2,1)S(1)} %collective-permute-done.5), channel_id=1, source_target_pairs={{0,112},{16,0},{32,16},{48,32},{64,48},{80,64},{96,80},{112,96},{1... | collective-permute-start | bytes 12296 | tf_op jit(solution)/shard_map/ppermute | solution.py:18
  64.7 12.6 %copy-start.2 = (bf16[8,3,896]{2,0,1:T(8,128)(2,1)S(1)}, bf16[8,3,896]{2,0,1:T(8,128)(2,1)}, u32[]{:S(2)}) copy-start(bf16[8,3,896]{2,0,1:T(8,128)(2,1)} %param.16) | copy-start | bytes 129028
  91.5 0.7 copy-start.4
  91.6 200.7 %all-gather.5.cloned.1.call-start = ((), (), s32[]{:S(2)}) async-start(), calls=%async_computation.4 | async-start | bytes 3899392 | tf_op jit(solution)/shard_map/all_gather | solution.py:121
  116.0 11.6 %copy-start.6 = (s32[2]{0:T(128)S(1)}, s32[2]{0:T(128)}, u32[]{:S(2)}) copy-start(s32[2]{0:T(128)} %param.18) | copy-start | bytes 28
  233.0 6.0 %slice-start = ((s8[7340032]{0:T(1024)(128)(4,1)}), s8[4194304]{0:T(1024)(128)(4,1)S(1)}, s32[]{:S(2)}) async-start(s8[7340032]{0:T(1024)(128)(4,1)} %bitcast.60), calls=%async_computation.6 | async-start | bytes 8388608
  233.0 5.9 %slice-start.1 = ((s8[7340032]{0:T(1024)(128)(4,1)}), s8[3145728]{0:T(1024)(128)(4,1)S(1)}, s32[]{:S(2)}) async-start(s8[7340032]{0:T(1024)(128)(4,1)} %bitcast.60), calls=%async_computation.7 | async-start | bytes 6291456
  242.8 98.1 %reduce-scatter.5.cloned.1.call-start = ((), (), s32[]{:S(2)}) async-start(), calls=%async_computation.5 | async-start | bytes 1032192 | tf_op jit(solution)/shard_map/reduce_scatter | solution.py:122
  242.9 62.5 %copy-start.7 = (bf16[896,224]{0,1:T(8,128)(2,1)S(1)}, bf16[896,224]{0,1:T(8,128)(2,1)}, u32[]{:S(2)}) copy-start(bf16[896,224]{0,1:T(8,128)(2,1)} %param.21) | copy-start | bytes 1204228
  292.2 48.6 %copy-start.1 = (bf16[7168,128]{1,0:T(8,128)(2,1)S(1)}, bf16[7168,128]{1,0:T(8,128)(2,1)}, u32[]{:S(2)}) copy-start(bf16[7168,128]{1,0:T(8,128)(2,1)} %param.15) | copy-start | bytes 5505028
  305.3 4.4 %copy-start.5 = (s32[2,8]{1,0:T(2,128)S(1)}, s32[2,8]{1,0:T(2,128)}, u32[]{:S(2)}) copy-start(s32[2,8]{1,0:T(2,128)} %param.20) | copy-start | bytes 196
Sparse Core Ops, SparseCore 0:
  17.8 28.3 all-gather.2
  91.7 138.4 reduce-scatter.2
  242.9 49.2 all-gather.4
  309.8 31.0 reduce-scatter.4
